TPU v7x, 32 devices: a whole 2x2x4 slice. The times are simulated.
32 devices in a mesh: wide: 16 (over z, y, core), narrow: 2 (over x).
Axes of the slice: x: 2, y: 2, z: 4, core: 2. Of those that a mesh axis runs over, the one named last changes fastest.
Arguments:
- users: float32 [49152, 256], P(('wide', 'narrow')), may hold values from -1.5 to 1.5
- user_state: float32 [49152], P(('wide', 'narrow')), may hold values from 0.05 to 0.5
- items: float32 [8192, 256], P('wide'), may hold values from -1.5 to 1.5
- item_state: float32 [8192], P('wide'), may hold values from 0.05 to 0.5
- tile_ids: int32 [16, 2, 2, 16], P('wide', 'narrow'), may hold values from 0 to 47, as said below
- tile_count: int32 [16, 2, 2], P('wide', 'narrow'), may hold values from 1 to 16, as said below
- pos_items: int32 [16, 2, 2, 16, 128], P('wide', 'narrow'), may hold values from 0 to 127
- neg_offsets: int32 [16, 2, 2, 16], P('wide', 'narrow'), may hold values from 0 to 384
Outputs:
- new_users: float32 [49152, 256], P(('wide', 'narrow'))
- new_user_state: float32 [49152], P(('wide', 'narrow'))
- new_items: float32 [8192, 256], P('wide')
- new_item_state: float32 [8192], P('wide')
Inputs may be any that keep to these rules, and one draw needn't show every extreme that they name: `tile_ids`: within one list the 16 ids are distinct tile numbers; slots at or after the count are ignored. `tile_count`: some entry equals 16.
All inputs are finite; a program needn't handle non-finite values.
Results may differ from a plain program's by a relative error of at most 0.0003.
Values sent between devices are 32-bit elements; how exact they have to be, the bound alone decides.
A program may use at most 64 MiB of HBM per device.

v0:
```python
import functools

import jax
import jax.numpy as jnp
from jax import lax
from jax.experimental import pallas as pl
from jax.experimental.pallas import tpu as pltpu
from jax.sharding import PartitionSpec as P

TILE = 128
STRATA = 2
BATCH = 4
CHUNKS = 8
AHEAD = 8
LAG_FRESH = 4
LAG_RELAY = 6
WINDOW = TILE + 16
MESH = pl.DeviceIdType.MESH
step_rate = 0.25
f32 = jnp.float32
bf16 = jnp.bfloat16
VMEM = pltpu.MemorySpace.VMEM
SMEM = pltpu.MemorySpace.SMEM


def dot(a, b, dims):
    return lax.dot_general(a, b, (dims, ((), ())), preferred_element_type=f32)


def pair(x):
    high = x.astype(bf16)
    low = (x - high.astype(f32)).astype(bf16)
    return jnp.concatenate([high, low], axis=0)


def tiles_kernel(
    stratum, ids, count, offsets, positives, users, state, block, negatives,
    new_users, new_state, pos_grad, neg_grad, split, square, padded, spread,
):
    cols = block.shape[0] // TILE
    rows = users.shape[0] // TILE
    side = TILE
    width = users.shape[1]
    new_users[...] = jnp.zeros(new_users.shape, f32)
    pos_grad[...] = jnp.zeros(pos_grad.shape, f32)
    spread[...] = jnp.zeros(spread.shape, f32)
    length = negatives.shape[0]
    padded[0:length, :] = negatives[...]
    padded[length:, :] = jnp.zeros((padded.shape[0] - length, width), f32)
    for col in range(cols):
        split[col] = pair(block[col * side : (col + 1) * side, :])
    live_count = count[0, stratum]
    item = lax.broadcasted_iota(jnp.int32, (side, side), 0)
    place = lax.broadcasted_iota(jnp.int32, (side, WINDOW), 1)

    def batch(step, carry):
        work = []
        for lane in range(BATCH):
            slot = step * BATCH + lane
            tile = ids[stratum, slot]
            within = lax.rem(offsets[stratum, slot], 8)
            window = pl.ds(pl.multiple_of(offsets[stratum, slot] - within, 8), WINDOW)
            row = pl.multiple_of(lax.div(tile, cols) * side, side)
            col = lax.rem(tile, cols)
            live = jnp.where(slot < live_count, 1.0 / side, 0.0).astype(f32)
            factors = users[pl.ds(row, side), :]
            factors_low = factors.astype(bf16)
            neg_rows = padded[window, :].astype(bf16)
            hot = jnp.where(item == positives[stratum, pl.ds(slot, 1), :], 1.0, 0.0).astype(f32)
            hot_t = hot.T.astype(bf16)
            hot = hot.astype(bf16)
            pos_rows = dot(jnp.concatenate([hot_t, hot_t], axis=1), split[col], ((1,), (0,)))
            neg_score = dot(factors_low, neg_rows, ((1,), (1,)))
            pos_score = jnp.sum(factors * pos_rows, axis=-1, keepdims=True)
            chosen = jnp.logical_and(place >= within, place < within + side)
            coeffs = jnp.where(chosen, live, 0.0) / (1.0 + jnp.exp(pos_score - neg_score))
            totals = jnp.sum(coeffs, axis=-1, keepdims=True)
            coeffs_low = coeffs.astype(bf16)
            factor_grad = dot(coeffs_low, neg_rows, ((1,), (0,))) - totals * pos_rows
            positive = dot(
                jnp.concatenate([hot, hot], axis=1), pair(totals * factors), ((1,), (0,))
            )
            negative = dot(coeffs.T.astype(bf16), factors_low, ((1,), (0,)))
            work.append((row, col, window, factor_grad, positive, negative))
        for row, col, window, factor_grad, positive, negative in work:
            new_users[pl.ds(row, side), :] += factor_grad
            at = pl.ds(pl.multiple_of(col * side, side), side)
            pos_grad[at, :] -= positive
            spread[window, :] += negative
        return carry

    lax.fori_loop(0, lax.div(live_count + (BATCH - 1), BATCH), batch, 0)
    neg_grad[...] = spread[0:length, :]
    square[...] = jnp.zeros(square.shape, f32)
    square[0:rows, :] = state[...]
    sums = square[...].T
    for row in range(rows):
        at = slice(row * side, (row + 1) * side)
        grad = new_users[at, :]
        fresh = sums[:, row : row + 1] + jnp.sum(grad * grad, axis=-1, keepdims=True) * (1.0 / width)
        new_users[at, :] = users[at, :] - (step_rate / jnp.sqrt(fresh)) * grad
        square[:, row : row + 1] = fresh
    new_state[...] = square[...].T[0:rows, :]


def run_tiles(stratum, ids, count, offsets, positives, users, state, block, negatives):
    width = users.shape[1]
    cols = block.shape[0] // TILE
    return pl.pallas_call(
        functools.partial(tiles_kernel, stratum),
        out_shape=(
            jax.ShapeDtypeStruct(users.shape, f32),
            jax.ShapeDtypeStruct(state.shape, f32),
            jax.ShapeDtypeStruct(block.shape, f32),
            jax.ShapeDtypeStruct(block.shape, f32),
        ),
        in_specs=[pl.BlockSpec(memory_space=SMEM)] * 3 + [pl.BlockSpec(memory_space=VMEM)] * 5,
        out_specs=(pl.BlockSpec(memory_space=VMEM),) * 4,
        scratch_shapes=[
            pltpu.VMEM((cols, 2 * TILE, width), bf16),
            pltpu.VMEM((TILE, TILE), f32),
            pltpu.VMEM((block.shape[0] + 16, width), f32),
            pltpu.VMEM((block.shape[0] + 16, width), f32),
        ],
        compiler_params=pltpu.CompilerParams(vmem_limit_bytes=24 * 1024 * 1024),
        name="tiles",
    )(ids, count, offsets, positives, users, state, block, negatives)


def greet(devices):
    barrier = pltpu.get_barrier_semaphore()
    for device in devices:
        pl.semaphore_signal(barrier, inc=1, device_id=device, device_id_type=MESH)
    pl.semaphore_wait(barrier, len(devices))


def send(src, dst, sems, kind, chunk, device):
    copy = pltpu.make_async_remote_copy(
        src_ref=src,
        dst_ref=dst,
        send_sem=sems.at[0, kind, chunk],
        recv_sem=sems.at[1, kind, chunk],
        device_id=device,
        device_id_type=MESH,
    )
    copy.start()
    return copy


def fetch_kernel(wide, count, *refs):
    block, negatives = refs[0], refs[count]
    sems, local_sems = refs[2 * count + 1 :]
    w, r = lax.axis_index("wide"), lax.axis_index("narrow")
    across = (lax.rem(w + wide // 2, wide), r)
    beside = (w, 1 - r)
    greet([across, beside])
    copies = []
    half = block.shape[0] // 2
    size = half // CHUNKS
    far, near = [], []

    def part(chunk):
        return pl.ds(pl.multiple_of(r * half + chunk * size, size), size)

    for c in range(CHUNKS):
        far.append(send(block.at[part(c), :], negatives.at[part(c), :], sems, 0, c, across))
    for k in range(count):
        copies.append(pltpu.make_async_copy(refs[k], refs[count + 1 + k], local_sems.at[k]))
        copies[k].start()
    for c in range(CHUNKS):
        far[c].wait_recv()
        near.append(send(negatives.at[part(c), :], negatives.at[part(c), :], sems, 1, c, beside))
    for c in range(CHUNKS):
        far[c].wait_send()
        near[c].wait()
    for copy in copies:
        copy.wait()


def run_fetch(*arrays):
    count = len(arrays)
    shapes = [jax.ShapeDtypeStruct(array.shape, array.dtype) for array in (arrays[0],) + arrays]
    return pl.pallas_call(
        functools.partial(fetch_kernel, lax.axis_size("wide"), count),
        out_shape=shapes,
        in_specs=[pl.BlockSpec(memory_space=pltpu.MemorySpace.HBM)] * count,
        out_specs=[pl.BlockSpec(memory_space=VMEM)] * (count + 1),
        scratch_shapes=[
            pltpu.SemaphoreType.DMA((2, 2, CHUNKS)),
            pltpu.SemaphoreType.DMA((count,)),
        ],
        compiler_params=pltpu.CompilerParams(
            collective_id=0, has_side_effects=True, vmem_limit_bytes=8 * 1024 * 1024
        ),
        name="fetch",
    )(*[pltpu.with_memory_space_constraint(a, pltpu.MemorySpace.HBM) for a in arrays])


def exchange_kernel(wide, shifts, last, *refs):
    pos_grad, neg_grad, block, state = refs[:4]
    outs = refs[4 : 4 + len(shifts)]
    new_state = refs[4 + len(shifts)]
    beside_neg, beside_pos, across_neg, summed, fresh_half, fresh_state, square, sems = refs[
        5 + len(shifts) :
    ]
    w, r = lax.axis_index("wide"), lax.axis_index("narrow")
    across = (lax.rem(w + wide // 2, wide), r)
    beside = (w, 1 - r)
    targets = [(lax.rem(w + shift + wide, wide), r) for shift in shifts]
    sources = [(lax.rem(w - shift + wide, wide), r) for shift in shifts]
    greet([beside, across] + targets + sources)
    width = block.shape[1]
    half = block.shape[0] // 2
    size = half // CHUNKS
    side = TILE

    def part(which, chunk):
        return pl.ds(pl.multiple_of(which * half + chunk * size, size), size)

    def local(chunk):
        return slice(chunk * size, (chunk + 1) * size)

    side_neg, side_pos, far, relayed = [], [], [], []
    moved = [[] for shift in shifts]

    def send_neg(c):
        side_neg.append(
            send(neg_grad.at[part(1 - r, c), :], beside_neg.at[local(c), :], sems, 0, c, beside)
        )

    def send_pos(c):
        side_pos.append(
            send(pos_grad.at[part(1 - r, c), :], beside_pos.at[local(c), :], sems, 1, c, beside)
        )

    def send_sum(c):
        side_neg[c].wait_recv()
        summed[local(c), :] = neg_grad[part(r, c), :] + beside_neg[local(c), :]
        far.append(send(summed.at[local(c), :], across_neg.at[local(c), :], sems, 2, c, across))

    def send_fresh(c):
        side_pos[c].wait_recv()
        far[c].wait_recv()
        grad = pos_grad[part(r, c), :] + beside_pos[local(c), :] + across_neg[local(c), :]
        row, begin = c * size // side, c * size % side
        fresh = sums[begin : begin + size, row : row + 1] + jnp.sum(
            grad * grad, axis=-1, keepdims=True
        ) * (1.0 / width)
        fresh_half[local(c), :] = block[part(r, c), :] - (step_rate / jnp.sqrt(fresh)) * grad
        square[begin : begin + size, row : row + 1] = fresh
        for k in reversed(range(len(shifts))):
            moved[k].append(
                send(
                    fresh_half.at[local(c), :], outs[k].at[part(r, c), :], sems, 3 + k, c, targets[k]
                )
            )

    def relay(c):
        for k in range(len(shifts)):
            moved[k][c].wait_recv()
            relayed.append(
                send(outs[k].at[part(r, c), :], outs[k].at[part(r, c), :], sems, 5 + k, c, beside)
            )

    for c in range(AHEAD):
        send_neg(c)
    square[...] = jnp.zeros(square.shape, f32)
    square[0 : half // side, :] = state[r]
    sums = square[...].T
    state_moved = None
    for step in range(CHUNKS + LAG_RELAY):
        if step < CHUNKS:
            send_sum(step)
            if step + AHEAD < CHUNKS:
                send_neg(step + AHEAD)
            send_pos(step)
        if 0 <= step - LAG_FRESH < CHUNKS:
            send_fresh(step - LAG_FRESH)
            if step - LAG_FRESH == CHUNKS - 1:
                fresh_state[...] = square[...].T[0 : half // side, :]
                state_moved = send(fresh_state, new_state.at[r], sems, 7, 0, targets[0])
        if 0 <= step - LAG_RELAY:
            relay(step - LAG_RELAY)
    state_moved.wait_recv()
    if last:
        relayed.append(send(new_state.at[r], new_state.at[r], sems, 7, 1, beside))
    for copies in [side_neg, side_pos, far] + moved + [[state_moved]]:
        for copy in copies:
            copy.wait_send()
    for copy in relayed:
        copy.wait()


def run_exchange(shifts, last, pos_grad, neg_grad, block, state):
    half = (block.shape[0] // 2, block.shape[1])
    outs = (jax.ShapeDtypeStruct(block.shape, f32),) * len(shifts)
    return pl.pallas_call(
        functools.partial(exchange_kernel, lax.axis_size("wide"), shifts, last),
        out_shape=outs + (jax.ShapeDtypeStruct(state.shape, f32),),
        in_specs=[pl.BlockSpec(memory_space=VMEM)] * 4,
        out_specs=(pl.BlockSpec(memory_space=VMEM),) * (len(shifts) + 1),
        scratch_shapes=[pltpu.VMEM(half, f32)] * 5
        + [
            pltpu.VMEM(state.shape[1:], f32),
            pltpu.VMEM((TILE, TILE), f32),
            pltpu.SemaphoreType.DMA((2, 8, CHUNKS)),
        ],
        compiler_params=pltpu.CompilerParams(
            collective_id=2 if last else 1,
            has_side_effects=True,
            vmem_limit_bytes=12 * 1024 * 1024,
        ),
        name="exchange",
    )(pos_grad, neg_grad, block, state)


def passed_along(block, distance):
    size = lax.axis_size("wide")
    return lax.ppermute(block, "wide", [((i - distance) % size, i) for i in range(size)])


def general_exchange(shift, pos_grad, neg_grad, block, state):
    half = lax.axis_size("wide") // 2
    total = lax.psum(pos_grad + passed_along(neg_grad, half), "narrow")
    new_state = state + jnp.mean(total * total, axis=-1)
    block = block - step_rate * total / jnp.sqrt(new_state)[:, None]
    return passed_along((block, new_state), shift)


def per_device(users, user_state, items, item_state, tile_ids, tile_count, pos_items, neg_offsets):
    wide, narrow = lax.axis_size("wide"), lax.axis_size("narrow")
    ids, count = tile_ids[0, 0], tile_count[0]
    positives, offsets = pos_items[0, 0], neg_offsets[0, 0]
    own_state = user_state.reshape(-1, TILE)
    block, block_state = items, item_state
    paired = narrow == 2
    if paired:
        block_state = item_state.reshape(2, -1, TILE)
        negatives, block, users, own_state, positives, block_state, ids, count, offsets = run_fetch(
            block, users, own_state, positives, block_state, ids, count, offsets
        )
    else:
        negatives = passed_along(block, wide // 2)
    for stratum in range(STRATA):
        users, own_state, pos_grad, neg_grad = run_tiles(
            stratum, ids, count, offsets, positives, users, own_state, block, negatives
        )
        last = stratum + 1 == STRATA
        if paired:
            shifts = (1 - STRATA,) if last else (1, 1 + wide // 2)
            results = run_exchange(shifts, last, pos_grad, neg_grad, block, block_state)
            block, block_state = results[0], results[-1]
            negatives = results[1]
        else:
            block, block_state = general_exchange(
                1 - STRATA if last else 1, pos_grad, neg_grad, block, block_state
            )
            if not last:
                negatives = passed_along(block, wide // 2)
    return (users, own_state.reshape(user_state.shape), block, block_state.reshape(item_state.shape))


def solution(mesh):
    return jax.shard_map(
        per_device,
        mesh=mesh,
        in_specs=(
            P(("wide", "narrow"), None),
            P(("wide", "narrow")),
            P("wide", None),
            P("wide"),
            P("wide", "narrow", None, None),
            P("wide", "narrow", None),
            P("wide", "narrow", None, None, None),
            P("wide", "narrow", None, None),
        ),
        out_specs=(P(("wide", "narrow"), None), P(("wide", "narrow")), P("wide", None), P("wide")),
        check_vma=False,
    )
```

profile of v0, /device:TPU:0, one launch (start us, length us, event | category | flops | bytes accessed | tf_op | source)
XLA Modules:
  0.0 94.8 jit_solution(11203897283405372661)
XLA Ops:
  0.6 20.3 %fetch.1 = (f32[512,256]{1,0:T(8,128)S(1)}, f32[512,256]{1,0:T(8,128)S(1)}, f32[1536,256]{1,0:T(8,128)S(1)}, f32[12,128]{1,0:T(8,128)S(1)}, s32[2,16,128]{2,1,0:...) custom-call(f32[512,256]{1,0:T(8,128)} %refs_0_.1, ...), custom_call_target="tpu_custom_call" | custom-call | tf_op jit(solution)/shard_map/fetch/pallas_call | solution.py:183
  20.9 4.3 %tiles.2 = (f32[1536,256]{1,0:T(8,128)S(1)}, f32[12,128]{1,0:T(8,128)S(1)}, f32[512,256]{1,0:T(8,128)S(1)}, f32[512,256]{1,0:T(8,128)S(1)}) custom-call(s32[2,16]{1,0:T(2,128)S(1)} %get-tuple-element.26.ids, s32[1,2]{1,0:T(1,128)S(1)} %get-tuple-element.27.count, s32[2,16]{1,0:T(2,128)S(1)} %get-tuple-element.28.offsets, ...), custom_call_target="tpu_custom_call" | custom-call | tf_op jit(solution)/shard_map/tiles/pallas_call | solution.py:109
  25.2 39.4 %exchange.2 = (f32[512,256]{1,0:T(8,128)S(1)}, f32[512,256]{1,0:T(8,128)S(1)}, f32[2,2,128]{2,1,0:T(2,128)S(1)}) custom-call(f32[512,256]{1,0:T(8,128)S(1)} %get-tuple-element.36.refs_0_, f32[512,256]{1,0:T(8,128)S(1)} %get-tuple-element.37.refs_1_, f32[512,256]{1,0:T(8,128)S(1)} %get-tuple-element.32.block.refs_2_, f32[2,2,128]{2,1,0:T(2,128)S(1)} %get-tuple-element.38.refs_3_), custom_call_target="tpu_custom_call" | custom-call | tf_op jit(solution)/shard_map/exchange/pallas_call | solution.py:297
  64.6 7.2 %tiles.3 = (f32[1536,256]{1,0:T(8,128)}, f32[12,128]{1,0:T(8,128)}, f32[512,256]{1,0:T(8,128)S(1)}, f32[512,256]{1,0:T(8,128)S(1)}) custom-call(s32[2,16]{1,0:T(2,128)S(1)} %get-tuple-element.26.ids, s32[1,2]{1,0:T(1,128)S(1)} %get-tuple-element.27.count, s32[2,16]{1,0:T(2,128)S(1)} %get-tuple-element.28.offsets, ...), custom_call_target="tpu_custom_call" | custom-call | tf_op jit(solution)/shard_map/tiles/pallas_call | solution.py:109
  71.9 21.5 %exchange.3 = (f32[512,256]{1,0:T(8,128)S(1)}, f32[2,2,128]{2,1,0:T(2,128)S(1)}) custom-call(f32[512,256]{1,0:T(8,128)S(1)} %get-tuple-element.43.refs_0_, f32[512,256]{1,0:T(8,128)S(1)} %get-tuple-element.44.refs_1_, f32[512,256]{1,0:T(8,128)S(1)} %get-tuple-element.39.block.refs_2_, f32[2,2,128]{2,1,0:T(2,128)S(1)} %get-tuple-element.45.refs_3_), custom_call_target="tpu_custom_call" | custom-call | tf_op jit(solution)/shard_map/exchange/pallas_call | solution.py:297
  93.4 0.8 copy.14
  94.2 0.6 copy.15
where the time goes:
time: 94.6 us; the launch traced here: 94.8 us
  Pallas kernels  92.8 us (98%)
  local copies, waits for them, and re-layouts  1.37 us (1%)
    pallas_call x2, Pallas kernels, run_exchange(): pl.pallas_call(functools.partial(exchange_kernel, lax.axis_size('wide'),...  60.9 us
    pallas_call x1, Pallas kernels, run_fetch(): pl.pallas_call(functools.partial(fetch_kernel, lax.axis_size('wide'), cou...  20.3 us
    pallas_call x2, Pallas kernels, run_tiles(): pl.pallas_call(functools.partial(tiles_kernel, stratum), out_shape=(jax.S...  11.6 us

commit v1 on v0

--- a/solution.py
+++ b/solution.py
@@ -12,8 +12,8 @@
 BATCH = 4
 CHUNKS = 8
 AHEAD = 8
-LAG_FRESH = 4
-LAG_RELAY = 6
+LAG_FRESH = 5
+LAG_RELAY = 7
 WINDOW = TILE + 16
 MESH = pl.DeviceIdType.MESH
 step_rate = 0.25
@@ -80,7 +80,10 @@
             positive = dot(
                 jnp.concatenate([hot, hot], axis=1), pair(totals * factors), ((1,), (0,))
             )
-            negative = dot(coeffs.T.astype(bf16), factors_low, ((1,), (0,)))
+            coeffs_t = coeffs.T.astype(bf16)
+            negative = dot(
+                jnp.concatenate([coeffs_t, coeffs_t], axis=1), pair(factors), ((1,), (0,))
+            )
             work.append((row, col, window, factor_grad, positive, negative))
         for row, col, window, factor_grad, positive, negative in work:
             new_users[pl.ds(row, side), :] += factor_grad

time: 94.6 us -> 94.2 us (level)
  no operation moved by 1% of the time
where the time goes in v1:
time: 94.2 us; the launch traced here: 94.4 us
  Pallas kernels  92.4 us (98%)
  local copies, waits for them, and re-layouts  1.37 us (1%)
    pallas_call x2, Pallas kernels, run_exchange(): pl.pallas_call(functools.partial(exchange_kernel, lax.axis_size('wide'),...  60.6 us
    pallas_call x1, Pallas kernels, run_fetch(): pl.pallas_call(functools.partial(fetch_kernel, lax.axis_size('wide'), cou...  20.3 us
    pallas_call x2, Pallas kernels, run_tiles(): pl.pallas_call(functools.partial(tiles_kernel, stratum), out_shape=(jax.S...  11.6 us

profile of v1, /device:TPU:0, one launch (start us, length us, event | category | flops | bytes accessed | tf_op | source)
XLA Modules:
  0.0 94.4 jit_solution(8177908579313545114)
XLA Ops:
  0.6 20.3 %fetch.1 = (f32[512,256]{1,0:T(8,128)S(1)}, f32[512,256]{1,0:T(8,128)S(1)}, f32[1536,256]{1,0:T(8,128)S(1)}, f32[12,128]{1,0:T(8,128)S(1)}, s32[2,16,128]{2,1,0:...) custom-call(f32[512,256]{1,0:T(8,128)} %refs_0_.1, ...), custom_call_target="tpu_custom_call" | custom-call | tf_op jit(solution)/shard_map/fetch/pallas_call | solution.py:186
  20.9 6.1 %tiles.2 = (f32[1536,256]{1,0:T(8,128)S(1)}, f32[12,128]{1,0:T(8,128)S(1)}, f32[512,256]{1,0:T(8,128)S(1)}, f32[512,256]{1,0:T(8,128)S(1)}) custom-call(s32[2,16]{1,0:T(2,128)S(1)} %get-tuple-element.26.ids, s32[1,2]{1,0:T(1,128)S(1)} %get-tuple-element.27.count, s32[2,16]{1,0:T(2,128)S(1)} %get-tuple-element.28.offsets, ...), custom_call_target="tpu_custom_call" | custom-call | tf_op jit(solution)/shard_map/tiles/pallas_call | solution.py:112
  27.0 35.8 %exchange.2 = (f32[512,256]{1,0:T(8,128)S(1)}, f32[512,256]{1,0:T(8,128)S(1)}, f32[2,2,128]{2,1,0:T(2,128)S(1)}) custom-call(f32[512,256]{1,0:T(8,128)S(1)} %get-tuple-element.36.refs_0_, f32[512,256]{1,0:T(8,128)S(1)} %get-tuple-element.37.refs_1_, f32[512,256]{1,0:T(8,128)S(1)} %get-tuple-element.32.block.refs_2_, f32[2,2,128]{2,1,0:T(2,128)S(1)} %get-tuple-element.38.refs_3_), custom_call_target="tpu_custom_call" | custom-call | tf_op jit(solution)/shard_map/exchange/pallas_call | solution.py:300
  62.9 5.4 %tiles.3 = (f32[1536,256]{1,0:T(8,128)}, f32[12,128]{1,0:T(8,128)}, f32[512,256]{1,0:T(8,128)S(1)}, f32[512,256]{1,0:T(8,128)S(1)}) custom-call(s32[2,16]{1,0:T(2,128)S(1)} %get-tuple-element.26.ids, s32[1,2]{1,0:T(1,128)S(1)} %get-tuple-element.27.count, s32[2,16]{1,0:T(2,128)S(1)} %get-tuple-element.28.offsets, ...), custom_call_target="tpu_custom_call" | custom-call | tf_op jit(solution)/shard_map/tiles/pallas_call | solution.py:112
  68.3 24.7 %exchange.3 = (f32[512,256]{1,0:T(8,128)S(1)}, f32[2,2,128]{2,1,0:T(2,128)S(1)}) custom-call(f32[512,256]{1,0:T(8,128)S(1)} %get-tuple-element.43.refs_0_, f32[512,256]{1,0:T(8,128)S(1)} %get-tuple-element.44.refs_1_, f32[512,256]{1,0:T(8,128)S(1)} %get-tuple-element.39.block.refs_2_, f32[2,2,128]{2,1,0:T(2,128)S(1)} %get-tuple-element.45.refs_3_), custom_call_target="tpu_custom_call" | custom-call | tf_op jit(solution)/shard_map/exchange/pallas_call | solution.py:300
  93.1 0.8 copy.14
  93.8 0.6 copy.15
